TPU v7x, 32 devices: a whole 2x2x4 slice. The times are simulated.
32 devices in a mesh: strip: 8 (over z, x), col: 4 (over y, core).
Axes of the slice: x: 2, y: 2, z: 4, core: 2. Of those that a mesh axis runs over, the one named last changes fastest.
Arguments:
- net_box: int32 [32768, 4], P(('strip', 'col')), may hold values from 0 to 1023, as said below
- net_weight: float32 [32768], P(('strip', 'col')), may hold values from 0.5 to 2
- pin_bin: int32 [32768, 4, 2], P(('strip', 'col')), may hold values from 0 to 1023, as said below
- conv_first: bfloat16 [3, 3, 32, 3], replicated, may hold values from -1.25 to 1.25
- bias_first: float32 [32], replicated, may hold values from -3 to 3
- conv_second: bfloat16 [3, 3, 32, 32], replicated, may hold values from -0.375 to 0.375
- bias_second: float32 [32], replicated, may hold values from -3 to 3
- cotangent: bfloat16 [512, 32, 1024], P('col', None, 'strip'), may hold values from -6 to 6
Outputs:
- congestion: bfloat16 [512, 32, 1024], P('col', None, 'strip')
- net_grad: float32 [32768], P(('strip', 'col'))
Inputs may be any that keep to these rules, and one draw needn't show every extreme that they name: `net_box`: box n = (x0, x1, y0, y1) has x0 <= x1 < x0 + 16 and y0 <= y1 < y0 + 16; y0 lies in rows s * 128 to (s + 1) * 128 - 1, where s = n // 4096 is the strip whose devices hold net n. Some box is 16 bins tall and wide. `pin_bin`: every pin of net n lies in net n's box.
All inputs are finite; a program needn't handle non-finite values.
Results may differ from a plain program's by a relative error of at most 0.0054.
Values may be sent and summed in bfloat16 or wider, within the bound.
No kernel may reach another device: no remote copies, remote signals or barrier semaphores. Data moves between devices by JAX's collectives and lax.ppermute only.
A program may use at most 192 MiB of HBM per device.

v0:
```python
import math
import jax
import jax.numpy as jnp
from jax import lax
from jax.sharding import PartitionSpec as P


def from_behind(x, axis, by):
    size = lax.axis_size(axis)
    pairs = [(i, i + by) for i in range(size) if 0 <= i + by < size]
    return lax.ppermute(x, axis, pairs)


def with_halo(block, sides, width):
    for axis, dim in sides:
        count = lax.axis_size(axis)
        forward = [(i, i + 1) for i in range(count - 1)]
        backward = [(target, source) for source, target in forward]
        low = lax.ppermute(
            lax.slice_in_dim(block, block.shape[dim] - width, None, axis=dim), axis, forward
        )
        high = lax.ppermute(lax.slice_in_dim(block, 0, width, axis=dim), axis, backward)
        block = jnp.concatenate([low, block, high], axis=dim)
    return block


def silu_slope(pre_act):
    sigmoid = jax.nn.sigmoid(pre_act)
    return sigmoid * (1.0 + pre_act * (1.0 - sigmoid))


def conv_valid(padded, weights, out_cols, out_rows):
    summed = None
    for shift_row in range(3):
        for shift_col in range(3):
            window = padded[shift_col : shift_col + out_cols, :, shift_row : shift_row + out_rows]
            product = jnp.einsum(
                "oi,xiy->xoy",
                weights[shift_row, shift_col],
                window,
                preferred_element_type=jnp.float32,
            )
            summed = product if summed is None else summed + product
    return summed


def conv_back(padded, weights, out_cols, out_rows):
    summed = None
    for shift_row in range(3):
        for shift_col in range(3):
            window = padded[
                2 - shift_col : 2 - shift_col + out_cols,
                :,
                2 - shift_row : 2 - shift_row + out_rows,
            ]
            product = jnp.einsum(
                "oi,xoy->xiy",
                weights[shift_row, shift_col],
                window,
                preferred_element_type=jnp.float32,
            )
            summed = product if summed is None else summed + product
    return summed


def strip_factors(box_rows, weights, pin_list, first_row, span):
    row_ids = first_row + jnp.arange(2 * span, dtype=jnp.int32)
    top_row = box_rows[:, 2]
    bottom_row = box_rows[:, 3]
    inside = (top_row[:, None] <= row_ids[None, :]) & (row_ids[None, :] <= bottom_row[:, None])
    box_height = (bottom_row - top_row + 1).astype(jnp.float32)
    box_width = (box_rows[:, 1] - box_rows[:, 0] + 1).astype(jnp.float32)
    values = jnp.stack([weights / box_height, weights / box_width], axis=1).astype(jnp.bfloat16)
    row_factor = inside.astype(jnp.bfloat16).reshape(-1, 2, 1, span) * values[:, None, :, None]
    pin_rows = pin_list[:, :, 0].reshape(-1)
    pin_factor = (pin_rows[:, None] == row_ids[None, :]).astype(jnp.bfloat16).reshape(-1, 2, span)
    return (row_factor, pin_list[:, :, 1].reshape(-1), pin_factor)


def column_block(col_ids, left_col, right_col, row_factor, pin_col, pin_factor):
    net_cols = (
        (left_col[:, None] <= col_ids[None, :]) & (col_ids[None, :] <= right_col[:, None])
    ).astype(jnp.bfloat16)
    pin_cols = (pin_col[:, None] == col_ids[None, :]).astype(jnp.bfloat16)
    demand = jnp.einsum("nk,nhcr->khcr", net_cols, row_factor, preferred_element_type=jnp.float32)
    density = jnp.einsum("pk,phr->khr", pin_cols, pin_factor, preferred_element_type=jnp.float32)
    return jnp.concatenate([demand, density[:, :, None, :]], axis=2)


def shards(
    net_box, net_weight, pin_bin, conv_first, bias_first, conv_second, bias_second, cotangent
):
    tile_cols = cotangent.shape[0]
    span = cotangent.shape[2]
    net_total = net_box.shape[0]
    strip_index = lax.axis_index("strip")
    col_index = lax.axis_index("col")
    all_rows = span * lax.axis_size("strip")
    all_cols = tile_cols * lax.axis_size("col")
    first_row = strip_index * span
    pin_width = pin_bin.shape[1]
    packed = jnp.concatenate(
        [
            net_box.astype(jnp.float32),
            pin_bin.reshape(net_total, 2 * pin_width).astype(jnp.float32),
            net_weight[:, None],
        ],
        axis=1,
    )
    own_cols = col_index * tile_cols + jnp.arange(tile_cols, dtype=jnp.int32)
    start_terms = jnp.zeros((tile_cols, 2, 3, span), jnp.float32)
    shard_piece = lax.all_gather(packed, "col", axis=0, tiled=True)
    piece_rows = shard_piece.shape[0]
    block_size = math.gcd(piece_rows, 1024)
    grouped = shard_piece.reshape(piece_rows // block_size, block_size, shard_piece.shape[1])

    def one_group(summed, net_group):
        box_rows = net_group[:, :4].astype(jnp.int32)
        pin_list = (
            net_group[:, 4 : 4 + 2 * pin_width].reshape(block_size, pin_width, 2).astype(jnp.int32)
        )
        weights = net_group[:, 4 + 2 * pin_width]
        row_factor, pin_col, pin_factor = strip_factors(
            box_rows, weights, pin_list, first_row, span
        )
        return (
            summed
            + column_block(
                own_cols, box_rows[:, 0], box_rows[:, 1], row_factor, pin_col, pin_factor
            ),
            None,
        )

    summed, unused = lax.scan(one_group, start_terms, grouped)
    spilled = from_behind(summed[:, 1].astype(jnp.bfloat16), "strip", 1).astype(jnp.float32)
    features = (summed[:, 0] + spilled).astype(jnp.bfloat16)
    stacked = jnp.concatenate([features, cotangent], axis=1)
    padded = with_halo(stacked, (("strip", 2), ("col", 0)), 2)
    in_channels = features.shape[1]
    col_ids = col_index * tile_cols - 1 + jnp.arange(tile_cols + 2, dtype=jnp.int32)
    row_ids = first_row - 1 + jnp.arange(span + 2, dtype=jnp.int32)
    inside = ((col_ids >= 0) & (col_ids < all_cols))[:, None, None] & (
        (row_ids >= 0) & (row_ids < all_rows)
    )[None, None, :]
    pre_act = (
        conv_valid(padded[:, :in_channels], conv_first, tile_cols + 2, span + 2)
        + bias_first[None, :, None]
    )
    hidden = jnp.where(inside, jax.nn.silu(pre_act), 0.0).astype(jnp.bfloat16)
    congestion = (
        conv_valid(hidden, conv_second, tile_cols, span) + bias_second[None, :, None]
    ).astype(jnp.bfloat16)
    back_hidden = conv_back(padded[:, in_channels:], conv_second, tile_cols + 2, span + 2)
    back_pre = jnp.where(inside, back_hidden * silu_slope(pre_act), 0.0).astype(jnp.bfloat16)
    back_maps = conv_back(back_pre, conv_first[:, :, :, :2], tile_cols, span).astype(jnp.bfloat16)
    from_below = from_behind(back_maps, "strip", -1)
    both_halves = jnp.stack([back_maps, from_below], axis=1).reshape(tile_cols, 4 * span)
    left_col = net_box[:, 0]
    right_col = net_box[:, 1]
    shard_piece = lax.all_gather(both_halves, "col", axis=0, tiled=True)
    piece_cols = jnp.arange(shard_piece.shape[0], dtype=jnp.int32)
    net_cols = (
        (left_col[:, None] <= piece_cols[None, :]) & (piece_cols[None, :] <= right_col[:, None])
    ).astype(jnp.bfloat16)
    column_sums = jnp.dot(net_cols, shard_piece, preferred_element_type=jnp.float32)
    column_sums = column_sums.reshape(net_total, 2, 2, span)
    net_rows = first_row + jnp.arange(2 * span, dtype=jnp.int32)
    in_rows = (
        (
            (net_box[:, 2][:, None] <= net_rows[None, :])
            & (net_rows[None, :] <= net_box[:, 3][:, None])
        )
        .astype(jnp.float32)
        .reshape(net_total, 2, span)
    )
    box_height = (net_box[:, 3] - net_box[:, 2] + 1).astype(jnp.float32)
    box_width = (right_col - left_col + 1).astype(jnp.float32)
    per_row = (
        column_sums[:, :, 0] / box_height[:, None, None]
        + column_sums[:, :, 1] / box_width[:, None, None]
    )
    net_grad = jnp.sum(in_rows * per_row, axis=(1, 2))
    return (congestion, net_grad)


def solution(mesh):
    placed = (
        P(("strip", "col"), None),
        P(("strip", "col")),
        P(("strip", "col"), None, None),
        P(),
        P(),
        P(),
        P(),
        P("col", None, "strip"),
    )
    return jax.shard_map(
        shards,
        mesh=mesh,
        in_specs=placed,
        out_specs=(P("col", None, "strip"), P(("strip", "col"))),
        check_vma=False,
    )
```

profile of v0, /device:TPU:19, one launch (start us, length us, event | category | flops | bytes accessed | tf_op | source)
XLA Modules:
  0.0 179.9 jit_solution(665664036078959381)
XLA Ops:
  2.9 6.3 %all_gather.6 = f32[4096,13]{0,1:T(8,128)S(1)} all-gather(f32[1024,13]{0,1:T(8,128)S(1)} %pad_maximum_fusion.10), channel_id=1, replica_groups=mesh['strip'=8,'col'=4] {'col'}, dimensions={0}, use_global_device_ids=true | all-gather | bytes 266240 | tf_op jit(solution)/shard_map/all_gather | solution.py:112
  9.4 13.7 %while.11 = (s32[]{:T(128)}, f32[128,2,3,128]{3,0,2,1:T(8,128)S(1)}, f32[4,1024,13]{1,0,2:T(4,128)S(1)}, s32[]{:T(128)}, s32[]{:T(128)}, /*index=5*/s32[]{:T(128)}, s32[]{:T(128)}) while((s32[]{:T(128)}, f32[128,2,3,128]{3,0,2,1:T(8,128)S(1)}, f32[4,1024,13]{1,0,2:T(4,128)S(1)}, s32[]{:T(128)}, s32[]{:T(128)}, ...), condition=%wide.region_1.2_spmd.clone, body=%wide.region_0.1_spmd.clone.sunk | while | flops 408091520 | bytes 3318379 | solution.py:134
  23.3 3.2 %collective-permute-start = (bf16[128,3,128]{0,2,1:T(8,128)(2,1)S(1)}, bf16[128,3,128]{0,2,1:T(8,128)(2,1)S(1)}, u32[]{:S(2)}, u32[]{:S(2)}) collective-permute-start(bf16[128,3,128]{0,2,1:T(8,128)(2,1)S(1)} %fusion.144), channel_id=1, source_target_pairs={{0,4},{4,8},{8,12},{12,16},{16,20},{20,24},{24,28},{1,5},{5,9},{9,... | collective-permute-start | bytes 294920 | tf_op jit(solution)/shard_map/ppermute | solution.py:11
  29.5 3.1 %collective-permute-start.2 = (bf16[128,35,2]{0,2,1:T(2,128)(2,1)S(1)}, bf16[128,35,2]{0,2,1:T(2,128)(2,1)S(1)}, u32[]{:S(2)}, u32[]{:S(2)}) collective-permute-start(bf16[128,35,2]{0,2,1:T(2,128)(2,1)S(1)} %get-tuple-element.87), channel_id=1, source_target_pairs={{4,0},{8,4},{12,8},{16,12},{20,16},{24,20},{28,24},{5,1},{9,5},{13... | collective-permute-start | bytes 53768 | tf_op jit(solution)/shard_map/ppermute | solution.py:22
  32.6 3.1 %collective-permute-start.1 = (bf16[128,35,2]{0,2,1:T(2,128)(2,1)S(1)}, bf16[128,35,2]{0,2,1:T(2,128)(2,1)S(1)}, u32[]{:S(2)}, u32[]{:S(2)}) collective-permute-start(bf16[128,35,2]{0,2,1:T(2,128)(2,1)S(1)} %get-tuple-element.86), channel_id=1, source_target_pairs={{0,4},{4,8},{8,12},{12,16},{16,20},{20,24},{24,28},{1,5},{5,9},{9,... | collective-permute-start | bytes 53768 | tf_op jit(solution)/shard_map/ppermute | solution.py:19
  38.7 3.6 %copy.58 = bf16[128,35,132]{2,1,0:T(8,128)(2,1)S(1)} copy(bf16[128,35,132]{0,2,1:T(8,128)(2,1)} %pad_maximum_fusion.8) | data formatting | bytes 2365440 | tf_op jit(solution)/shard_map/concatenate | solution.py:23
  42.3 5.4 %collective-permute-start.3 = (bf16[2,35,132]{2,1,0:T(8,128)(2,1)S(1)}, bf16[2,35,132]{2,1,0:T(8,128)(2,1)S(1)}, u32[]{:S(2)}, u32[]{:S(2)}) collective-permute-start(bf16[2,35,132]{2,1,0:T(8,128)(2,1)S(1)} %get-tuple-element.84), channel_id=1, source_target_pairs={{0,1},{1,2},{2,3},{4,5},{5,6},{6,7},{8,9},{9,10},{10,11},{12,13},{... | collective-permute-start | bytes 55448 | tf_op jit(solution)/shard_map/ppermute | solution.py:19
  53.1 2.9 %fusion.104 = f32[130,130,32]{1,2,0:T(8,128)} fusion(bf16[2,35,132]{2,1,0:T(8,128)(2,1)S(1)} %collective-permute-done.4, bf16[128,35,132]{2,1,0:T(8,128)(2,1)S(1)} %copy.58, bf16[2,35,132]{2,1,0:T(8,128)(2,1)S(1)} %collective-permute-done.3, bf16[3,3,32,3]{2,3,1,0:T(4,128)(2,1)S(1)} %copy-done.10), kind=kOutput, calls=%fused_computation.133 | convolution fusion | flops 3549000 | bytes 4867584 | tf_op jit(solution)/shard_map/oi,xiy->xoy/dot_general | solution.py:37
  56.0 2.8 %fusion.114 = f32[130,130,32]{1,2,0:T(8,128)} fusion(bf16[2,35,132]{2,1,0:T(8,128)(2,1)S(1)} %collective-permute-done.4, bf16[128,35,132]{2,1,0:T(8,128)(2,1)S(1)} %copy.58, bf16[3,3,32,3]{2,3,1,0:T(4,128)(2,1)S(1)} %copy-done.10), kind=kOutput, calls=%fused_computation.143 | convolution fusion | flops 3447600 | bytes 4826624 | tf_op jit(solution)/shard_map/oi,xiy->xoy/dot_general | solution.py:37
  58.8 2.8 %fusion.118 = f32[130,130,32]{1,2,0:T(8,128)} fusion(bf16[2,35,132]{2,1,0:T(8,128)(2,1)S(1)} %collective-permute-done.4, bf16[128,35,132]{2,1,0:T(8,128)(2,1)S(1)} %copy.58, bf16[2,35,132]{2,1,0:T(8,128)(2,1)S(1)} %collective-permute-done.3, bf16[3,3,32,3]{2,3,1,0:T(4,128)(2,1)S(1)} %copy-done.10), kind=kOutput, calls=%fused_computation.147 | convolution fusion | flops 3549000 | bytes 4867584 | tf_op jit(solution)/shard_map/oi,xiy->xoy/dot_general | solution.py:37
  67.0 2.8 %fusion.138 = f32[130,130,32]{1,2,0:T(8,128)} fusion(bf16[128,35,132]{2,1,0:T(8,128)(2,1)S(1)} %copy.58, bf16[2,35,132]{2,1,0:T(8,128)(2,1)S(1)} %collective-permute-done.3, bf16[3,3,32,3]{2,3,1,0:T(4,128)(2,1)S(1)} %copy-done.10), kind=kOutput, calls=%fused_computation.167 | convolution fusion | flops 3447600 | bytes 4826624 | tf_op jit(solution)/shard_map/oi,xiy->xoy/dot_general | solution.py:37
  69.8 2.8 %fusion.132 = f32[130,130,32]{1,2,0:T(8,128)} fusion(bf16[2,35,132]{2,1,0:T(8,128)(2,1)S(1)} %collective-permute-done.4, bf16[128,35,132]{2,1,0:T(8,128)(2,1)S(1)} %copy.58, bf16[2,35,132]{2,1,0:T(8,128)(2,1)S(1)} %collective-permute-done.3, bf16[3,3,32,3]{2,3,1,0:T(4,128)(2,1)S(1)} %copy-done.10), kind=kOutput, calls=%fused_computation.161 | convolution fusion | flops 3549000 | bytes 4867584 | tf_op jit(solution)/shard_map/oi,xiy->xoy/dot_general | solution.py:37
  72.6 14.8 %fusion.34 = (bf16[130,32,130]{2,1,0:T(8,128)(2,1)S(1)}, f32[130,130,32]{1,2,0:T(8,128)}) fusion(pred[130,130]{1,0:T(8,128)(4,1)S(1)} %broadcast_and_fusion, f32[32]{0:T(128)S(1)} %copy-done.12, bf16[3,3,32,3]{2,3,1,0:T(4,128)(2,1)S(1)} %copy-done.10, bf16[2,35,132]{2,1,0:T(8,128)(2,1)S(1)} %collective-permute-done.4, bf16[128,35,132]{2,1,0:T(8,128)(2,1)S(1)} %copy.58, ...), kind=kOutput, calls=%fused_computation.44 | convolution fusion | flops 11559600 | bytes 23249152 | tf_op jit(solution)/shard_map/oi,xiy->xoy/dot_general | solution.py:37
  105.3 3.1 %fusion.55 = f32[130,130,32]{1,2,0:T(8,128)} fusion(bf16[132,35,132]{2,1,0:T(8,128)(2,1)S(1)} %pad_maximum_fusion.1, bf16[3,3,32,32]{3,2,1,0:T(8,128)(2,1)S(1)} %copy-done.8), kind=kOutput, calls=%fused_computation.73 | convolution fusion | flops 34611200 | bytes 4301312 | tf_op jit(solution)/shard_map/oi,xoy->xiy/dot_general | solution.py:56
  108.5 3.2 %fusion.57 = f32[130,130,32]{1,2,0:T(8,128)} fusion(bf16[132,35,132]{2,1,0:T(8,128)(2,1)S(1)} %pad_maximum_fusion.1, bf16[3,3,32,32]{3,2,1,0:T(8,128)(2,1)S(1)} %copy-done.8), kind=kOutput, calls=%fused_computation.75 | convolution fusion | flops 34611200 | bytes 4301312 | tf_op jit(solution)/shard_map/oi,xoy->xiy/dot_general | solution.py:56
  111.6 2.8 %fusion.53 = f32[130,130,32]{1,2,0:T(8,128)} fusion(bf16[2,35,132]{2,1,0:T(8,128)(2,1)S(1)} %collective-permute-done.4, bf16[128,35,132]{2,1,0:T(8,128)(2,1)S(1)} %copy.58, bf16[3,3,32,32]{3,2,1,0:T(8,128)(2,1)S(1)} %copy-done.8), kind=kOutput, calls=%fused_computation.71 | convolution fusion | flops 36774400 | bytes 4833792 | tf_op jit(solution)/shard_map/oi,xoy->xiy/dot_general | solution.py:56
  114.5 3.6 %fusion.44 = f32[130,130,32]{1,2,0:T(8,128)} fusion(bf16[128,35,132]{2,1,0:T(8,128)(2,1)S(1)} %copy.58, bf16[2,35,132]{2,1,0:T(8,128)(2,1)S(1)} %collective-permute-done.3, bf16[3,3,32,32]{3,2,1,0:T(8,128)(2,1)S(1)} %copy-done.8), kind=kOutput, calls=%fused_computation.62 | convolution fusion | flops 35152000 | bytes 4833792 | tf_op jit(solution)/shard_map/oi,xoy->xiy/dot_general | solution.py:56
  118.1 3.6 %fusion.38 = f32[130,130,32]{1,2,0:T(8,128)} fusion(bf16[128,35,132]{2,1,0:T(8,128)(2,1)S(1)} %copy.58, bf16[2,35,132]{2,1,0:T(8,128)(2,1)S(1)} %collective-permute-done.4, bf16[3,3,32,32]{3,2,1,0:T(8,128)(2,1)S(1)} %copy-done.8), kind=kOutput, calls=%fused_computation.58 | convolution fusion | flops 35152000 | bytes 4833792 | tf_op jit(solution)/shard_map/oi,xoy->xiy/dot_general | solution.py:56
  121.7 3.9 %fusion.47 = f32[130,130,32]{1,2,0:T(8,128)} fusion(bf16[128,35,132]{2,1,0:T(8,128)(2,1)S(1)} %copy.58, bf16[2,35,132]{2,1,0:T(8,128)(2,1)S(1)} %collective-permute-done.3, bf16[3,3,32,32]{3,2,1,0:T(8,128)(2,1)S(1)} %copy-done.8), kind=kOutput, calls=%fused_computation.64 | convolution fusion | flops 35152000 | bytes 4833792 | tf_op jit(solution)/shard_map/oi,xoy->xiy/dot_general | solution.py:56
  125.7 3.7 %fusion.41 = f32[130,130,32]{1,2,0:T(8,128)} fusion(bf16[128,35,132]{2,1,0:T(8,128)(2,1)S(1)} %copy.58, bf16[2,35,132]{2,1,0:T(8,128)(2,1)S(1)} %collective-permute-done.4, bf16[3,3,32,32]{3,2,1,0:T(8,128)(2,1)S(1)} %copy-done.8), kind=kOutput, calls=%fused_computation.60 | convolution fusion | flops 35152000 | bytes 4833792 | tf_op jit(solution)/shard_map/oi,xoy->xiy/dot_general | solution.py:56
  129.4 15.3 %fusion.29 = bf16[130,32,130]{2,1,0:T(8,128)(2,1)} fusion(f32[130,130,32]{1,2,0:T(8,128)} %get-tuple-element.93, f32[130,130,32]{1,2,0:T(8,128)} %fusion.51, f32[130,130,32]{1,2,0:T(8,128)} %fusion.53, f32[130,130,32]{1,2,0:T(8,128)} %fusion.44, f32[130,130,32]{1,2,0:T(8,128)} %fusion.55, f32[130,130,32]{1,2,0:T(8,128)} %fusion.38, ...), kind=kOutput, calls=%fused_computation.36 | convolution fusion | flops 46508800 | bytes 23255808 | tf_op jit(solution)/shard_map/oi,xoy->xiy/dot_general | solution.py:56
  162.3 3.0 %collective-permute-start.5 = (bf16[128,2,128]{2,1,0:T(2,128)(2,1)S(1)}, bf16[128,2,128]{2,1,0:T(2,128)(2,1)S(1)}, u32[]{:S(2)}, u32[]{:S(2)}) collective-permute-start(bf16[128,2,128]{2,1,0:T(2,128)(2,1)S(1)} %bitcast.290), channel_id=1, source_target_pairs={{4,0},{8,4},{12,8},{16,12},{20,16},{24,20},{28,24},{5,1},{9,5},{13... | collective-permute-start | bytes 196616 | tf_op jit(solution)/shard_map/ppermute | solution.py:11
  165.4 4.2 %fusion.62 = bf16[128,32,128]{2,1,0:T(8,128)(2,1)} fusion(f32[128,128,32]{1,2,0:T(8,128)S(1)} %copy-done, f32[128,128,32]{1,2,0:T(8,128)S(1)} %copy-done.1, f32[128,128,32]{1,2,0:T(8,128)S(1)} %copy-done.2, f32[128,128,32]{1,2,0:T(8,128)S(1)} %copy-done.3, f32[128,128,32]{1,2,0:T(8,128)S(1)} %copy-done.4, f32[128,128,32]{1,2,0:T(8,128)S(1)} %copy-done.5, ...), kind=kOutput, calls=%fused_computation.82 | convolution fusion | flops 38797312 | bytes 18883072 | tf_op jit(solution)/shard_map/oi,xiy->xoy/dot_general | solution.py:37
  169.9 7.5 %all_gather.7 = bf16[512,512]{0,1:T(8,128)(2,1)S(1)} all-gather(bf16[128,512]{0,1:T(8,128)(2,1)S(1)} %bitcast.285), channel_id=1, replica_groups=mesh['strip'=8,'col'=4] {'col'}, dimensions={0}, use_global_device_ids=true | all-gather | bytes 655360 | tf_op jit(solution)/shard_map/all_gather | solution.py:160
  (153 shorter events, 70.6 us)
Async XLA Ops:
  9.3 17.3 %copy-start.9 = (s32[1024,4]{0,1:T(4,128)S(1)}, s32[1024,4]{0,1:T(4,128)}, u32[]{:S(2)}) copy-start(s32[1024,4]{0,1:T(4,128)} %param.10) | copy-start | bytes 49156
  9.3 17.3 %copy-start.7 = (bf16[128,32,128]{2,1,0:T(8,128)(2,1)S(1)}, bf16[128,32,128]{2,1,0:T(8,128)(2,1)}, u32[]{:S(2)}) copy-start(bf16[128,32,128]{2,1,0:T(8,128)(2,1)} %param.17) | copy-start | bytes 3145732
  23.3 6.1 %collective-permute-start = (bf16[128,3,128]{0,2,1:T(8,128)(2,1)S(1)}, bf16[128,3,128]{0,2,1:T(8,128)(2,1)S(1)}, u32[]{:S(2)}, u32[]{:S(2)}) collective-permute-start(bf16[128,3,128]{0,2,1:T(8,128)(2,1)S(1)} %fusion.144), channel_id=1, source_target_pairs={{0,4},{4,8},{8,12},{12,16},{16,20},{20,24},{24,28},{1,5},{5,9},{9,... | collective-permute-start | bytes 294920 | tf_op jit(solution)/shard_map/ppermute | solution.py:11
  29.5 6.2 %collective-permute-start.2 = (bf16[128,35,2]{0,2,1:T(2,128)(2,1)S(1)}, bf16[128,35,2]{0,2,1:T(2,128)(2,1)S(1)}, u32[]{:S(2)}, u32[]{:S(2)}) collective-permute-start(bf16[128,35,2]{0,2,1:T(2,128)(2,1)S(1)} %get-tuple-element.87), channel_id=1, source_target_pairs={{4,0},{8,4},{12,8},{16,12},{20,16},{24,20},{28,24},{5,1},{9,5},{13... | collective-permute-start | bytes 53768 | tf_op jit(solution)/shard_map/ppermute | solution.py:22
  32.6 4.5 %collective-permute-start.1 = (bf16[128,35,2]{0,2,1:T(2,128)(2,1)S(1)}, bf16[128,35,2]{0,2,1:T(2,128)(2,1)S(1)}, u32[]{:S(2)}, u32[]{:S(2)}) collective-permute-start(bf16[128,35,2]{0,2,1:T(2,128)(2,1)S(1)} %get-tuple-element.86), channel_id=1, source_target_pairs={{0,4},{4,8},{8,12},{12,16},{16,20},{20,24},{24,28},{1,5},{5,9},{9,... | collective-permute-start | bytes 53768 | tf_op jit(solution)/shard_map/ppermute | solution.py:19
  35.7 14.2 %copy-start.10 = (bf16[3,3,32,3]{2,3,1,0:T(4,128)(2,1)S(1)}, bf16[3,3,32,3]{2,3,1,0:T(4,128)(2,1)}, u32[]{:S(2)}) copy-start(bf16[3,3,32,3]{2,3,1,0:T(4,128)(2,1)} %param.13) | copy-start | bytes 5188
  42.3 7.6 %collective-permute-start.3 = (bf16[2,35,132]{2,1,0:T(8,128)(2,1)S(1)}, bf16[2,35,132]{2,1,0:T(8,128)(2,1)S(1)}, u32[]{:S(2)}, u32[]{:S(2)}) collective-permute-start(bf16[2,35,132]{2,1,0:T(8,128)(2,1)S(1)} %get-tuple-element.84), channel_id=1, source_target_pairs={{0,1},{1,2},{2,3},{4,5},{5,6},{6,7},{8,9},{9,10},{10,11},{12,13},{... | collective-permute-start | bytes 55448 | tf_op jit(solution)/shard_map/ppermute | solution.py:19
  47.8 5.3 %collective-permute-start.4 = (bf16[2,35,132]{2,1,0:T(8,128)(2,1)S(1)}, bf16[2,35,132]{2,1,0:T(8,128)(2,1)S(1)}, u32[]{:S(2)}, u32[]{:S(2)}) collective-permute-start(bf16[2,35,132]{2,1,0:T(8,128)(2,1)S(1)} %get-tuple-element.85), channel_id=1, source_target_pairs={{1,0},{2,1},{3,2},{5,4},{6,5},{7,6},{9,8},{10,9},{11,10},{13,12},{... | collective-permute-start | bytes 55448 | tf_op jit(solution)/shard_map/ppermute | solution.py:22
  69.8 2.8 %copy-start.12 = (f32[32]{0:T(128)S(1)}, f32[32]{0:T(128)}, u32[]{:S(2)}) copy-start(f32[32]{0:T(128)} %param.14) | copy-start | bytes 388
  72.6 14.8 %copy-start.8 = (bf16[3,3,32,32]{3,2,1,0:T(8,128)(2,1)S(1)}, bf16[3,3,32,32]{3,2,1,0:T(8,128)(2,1)}, u32[]{:S(2)}) copy-start(bf16[3,3,32,32]{3,2,1,0:T(8,128)(2,1)} %param.15) | copy-start | bytes 55300
  129.4 36.0 %copy-start.5 = (f32[128,128,32]{1,2,0:T(8,128)S(1)}, f32[128,128,32]{1,2,0:T(8,128)}, u32[]{:S(2)}) copy-start(f32[128,128,32]{1,2,0:T(8,128)} %fusion.89) | copy-start | bytes 6291460
  129.4 36.0 %copy-start.6 = (f32[128,128,32]{1,2,0:T(8,128)S(1)}, f32[128,128,32]{1,2,0:T(8,128)}, u32[]{:S(2)}) copy-start(f32[128,128,32]{1,2,0:T(8,128)} %fusion.93) | copy-start | bytes 6291460
  146.8 18.6 %copy-start.4 = (f32[128,128,32]{1,2,0:T(8,128)S(1)}, f32[128,128,32]{1,2,0:T(8,128)}, u32[]{:S(2)}) copy-start(f32[128,128,32]{1,2,0:T(8,128)} %fusion.87) | copy-start | bytes 6291460
  149.0 16.3 %copy-start.3 = (f32[128,128,32]{1,2,0:T(8,128)S(1)}, f32[128,128,32]{1,2,0:T(8,128)}, u32[]{:S(2)}) copy-start(f32[128,128,32]{1,2,0:T(8,128)} %fusion.85) | copy-start | bytes 6291460
  153.4 12.0 %copy-start.2 = (f32[128,128,32]{1,2,0:T(8,128)S(1)}, f32[128,128,32]{1,2,0:T(8,128)}, u32[]{:S(2)}) copy-start(f32[128,128,32]{1,2,0:T(8,128)} %fusion.83) | copy-start | bytes 6291460
  155.6 9.8 %copy-start = (f32[128,128,32]{1,2,0:T(8,128)S(1)}, f32[128,128,32]{1,2,0:T(8,128)}, u32[]{:S(2)}) copy-start(f32[128,128,32]{1,2,0:T(8,128)} %fusion.79) | copy-start | bytes 6291460
  155.6 9.8 %copy-start.1 = (f32[128,128,32]{1,2,0:T(8,128)S(1)}, f32[128,128,32]{1,2,0:T(8,128)}, u32[]{:S(2)}) copy-start(f32[128,128,32]{1,2,0:T(8,128)} %fusion.81) | copy-start | bytes 6291460
  155.6 9.8 %copy-start.11 = (f32[32]{0:T(128)S(1)}, f32[32]{0:T(128)}, u32[]{:S(2)}) copy-start(f32[32]{0:T(128)} %param.16) | copy-start | bytes 388
  162.3 7.3 %collective-permute-start.5 = (bf16[128,2,128]{2,1,0:T(2,128)(2,1)S(1)}, bf16[128,2,128]{2,1,0:T(2,128)(2,1)S(1)}, u32[]{:S(2)}, u32[]{:S(2)}) collective-permute-start(bf16[128,2,128]{2,1,0:T(2,128)(2,1)S(1)} %bitcast.290), channel_id=1, source_target_pairs={{4,0},{8,4},{12,8},{16,12},{20,16},{24,20},{28,24},{5,1},{9,5},{13... | collective-permute-start | bytes 196616 | tf_op jit(solution)/shard_map/ppermute | solution.py:11
where the time goes:
time: 181 us; the launch traced here: 180 us
  matrix products  124 us (69%)
  starting transfers between devices  19.9 us (11%)
  blocking collectives  13.8 us (8%)
  local copies, waits for them, and re-layouts  9.63 us (5%)
  other arithmetic  7.78 us (4%)
  waiting for transfers between devices  3.59 us (2%)
    dot_general x18, matrix products, conv_back(): jnp.einsum('oi,xoy->xiy', weights[shift_row, shift_col], window, preferre...  59.7 us
    dot_general x18, matrix products, conv_valid(): jnp.einsum('oi,xiy->xoy', weights[shift_row, shift_col], window, preferre...  55.9 us
    ppermute x2, starting transfers between devices, with_halo(): lax.ppermute(lax.slice_in_dim(block, block.shape[dim] - width, None, axis...  8.54 us
    all_gather x1, blocking collectives, shards(): shard_piece = lax.all_gather(both_halves, 'col', axis=0, tiled=True)  7.48 us
    all_gather x1, blocking collectives, shards(): shard_piece = lax.all_gather(packed, 'col', axis=0, tiled=True)  6.3 us
    ppermute x2, starting transfers between devices, from_behind(): return lax.ppermute(x, axis, pairs)  6.19 us
    ppermute x2, starting transfers between devices, with_halo(): lax.ppermute(lax.slice_in_dim(block, 0, width, axis=dim), axis, backward)  5.17 us
    dot_general x4, matrix products, column_block(): jnp.einsum('pk,phr->khr', pin_cols, pin_factor, preferred_element_type=jn...  4.31 us
  transfers between devices with their start and end apart: 6, of which 3 were waited for; matrix products, arithmetic and copies ran while one was open for 4% of the time, Pallas kernels for 0%

commit v1 on v0

--- a/solution.py
+++ b/solution.py
@@ -157,7 +157,15 @@
     both_halves = jnp.stack([back_maps, from_below], axis=1).reshape(tile_cols, 4 * span)
     left_col = net_box[:, 0]
     right_col = net_box[:, 1]
-    shard_piece = lax.all_gather(both_halves, "col", axis=0, tiled=True)
+    ways, here = (lax.axis_size("col"), lax.axis_index("col"))
+    grown, reach = (both_halves, 1)
+    while reach < ways:
+        theirs = lax.ppermute(grown, "col", [(d, d ^ reach) for d in range(ways)])
+        mine_first = jnp.concatenate([grown, theirs], axis=0)
+        theirs_first = jnp.concatenate([theirs, grown], axis=0)
+        grown = jnp.where(here & reach == 0, mine_first, theirs_first)
+        reach = 2 * reach
+    shard_piece = grown
     piece_cols = jnp.arange(shard_piece.shape[0], dtype=jnp.int32)
     net_cols = (
         (left_col[:, None] <= piece_cols[None, :]) & (piece_cols[None, :] <= right_col[:, None])

time: 181 us -> 164 us (0.906)
  matrix products: 124 us -> 111 us
  blocking collectives: 13.8 us -> 6.3 us
  starting transfers between devices: 19.9 us -> 22.4 us
    dot_general x18, matrix products: 59.7 us -> 44.4 us  [conv_back(): jnp.einsum('oi,xoy->xiy', weights[shift_row, shift_col], window, preferre...]
    all_gather x1 -> x0, blocking collectives: 7.48 us -> none  [shards(): shard_piece = lax.all_gather(both_halves, 'col', axis=0, tiled=True)]
    dot_general x18, matrix products: 55.9 us -> 59 us  [conv_valid(): jnp.einsum('oi,xiy->xoy', weights[shift_row, shift_col], window, preferre...]
    ppermute x0 -> x2, starting transfers between devices: none -> 2.54 us  [shards(): theirs = lax.ppermute(grown, 'col', [(d, d ^ reach) for d in range(ways)])]
  transfers between devices with their start and end apart: 6 -> 8, of which waited for: 3 -> 4; matrix products, arithmetic and copies ran while one was open for 4% -> 9% of each run, Pallas kernels for 0% -> 0%
where the time goes in v1:
time: 164 us
  matrix products  111 us (68%)
  starting transfers between devices  22.4 us (14%)
  local copies, waits for them, and re-layouts  9.61 us (6%)
  other arithmetic  7.9 us (5%)
  blocking collectives  6.3 us (4%)
  waiting for transfers between devices  4.73 us (3%)
    dot_general x18, matrix products, conv_valid(): jnp.einsum('oi,xiy->xoy', weights[shift_row, shift_col], window, preferre...  59 us
    dot_general x18, matrix products, conv_back(): jnp.einsum('oi,xoy->xiy', weights[shift_row, shift_col], window, preferre...  44.4 us
    ppermute x2, starting transfers between devices, with_halo(): lax.ppermute(lax.slice_in_dim(block, block.shape[dim] - width, None, axis...  8.55 us
    all_gather x1, blocking collectives, shards(): shard_piece = lax.all_gather(packed, 'col', axis=0, tiled=True)  6.3 us
    ppermute x2, starting transfers between devices, from_behind(): return lax.ppermute(x, axis, pairs)  6.18 us
    ppermute x2, starting transfers between devices, with_halo(): lax.ppermute(lax.slice_in_dim(block, 0, width, axis=dim), axis, backward)  5.17 us
    dot_general x4, matrix products, column_block(): jnp.einsum('pk,phr->khr', pin_cols, pin_factor, preferred_element_type=jn...  4.31 us
    concatenate x1, local copies, waits for them, and re-layouts, with_halo(): block = jnp.concatenate([low, block, high], axis=dim)  3.6 us
  transfers between devices with their start and end apart: 8, of which 4 were waited for; matrix products, arithmetic and copies ran while one was open for 9% of the time, Pallas kernels for 0%

profile of v1, /device:TPU:19, one launch (start us, length us, event | category | flops | bytes accessed | tf_op | source)
XLA Modules:
  0.0 163.7 jit_solution(18188064012344319711)
XLA Ops:
  2.9 6.3 %all_gather.3 = f32[4096,13]{0,1:T(8,128)S(1)} all-gather(f32[1024,13]{0,1:T(8,128)S(1)} %pad_maximum_fusion.10), channel_id=1, replica_groups=mesh['strip'=8,'col'=4] {'col'}, dimensions={0}, use_global_device_ids=true | all-gather | bytes 266240 | tf_op jit(solution)/shard_map/all_gather | solution.py:112
  9.4 13.7 %while.11 = (s32[]{:T(128)}, f32[128,2,3,128]{3,0,2,1:T(8,128)S(1)}, f32[4,1024,13]{1,0,2:T(4,128)S(1)}, s32[]{:T(128)}, s32[]{:T(128)}, /*index=5*/s32[]{:T(128)}, s32[]{:T(128)}) while((s32[]{:T(128)}, f32[128,2,3,128]{3,0,2,1:T(8,128)S(1)}, f32[4,1024,13]{1,0,2:T(4,128)S(1)}, s32[]{:T(128)}, s32[]{:T(128)}, ...), condition=%wide.region_1.2_spmd.clone, body=%wide.region_0.1_spmd.clone.sunk | while | flops 408091520 | bytes 3318379 | solution.py:134
  23.3 3.2 %collective-permute-start = (bf16[128,3,128]{0,2,1:T(8,128)(2,1)S(1)}, bf16[128,3,128]{0,2,1:T(8,128)(2,1)S(1)}, u32[]{:S(2)}, u32[]{:S(2)}) collective-permute-start(bf16[128,3,128]{0,2,1:T(8,128)(2,1)S(1)} %fusion.150), channel_id=1, source_target_pairs={{0,4},{4,8},{8,12},{12,16},{16,20},{20,24},{24,28},{1,5},{5,9},{9,... | collective-permute-start | bytes 294920 | tf_op jit(solution)/shard_map/ppermute | solution.py:11
  29.5 3.1 %collective-permute-start.2 = (bf16[128,35,2]{0,2,1:T(2,128)(2,1)S(1)}, bf16[128,35,2]{0,2,1:T(2,128)(2,1)S(1)}, u32[]{:S(2)}, u32[]{:S(2)}) collective-permute-start(bf16[128,35,2]{0,2,1:T(2,128)(2,1)S(1)} %get-tuple-element.87), channel_id=1, source_target_pairs={{4,0},{8,4},{12,8},{16,12},{20,16},{24,20},{28,24},{5,1},{9,5},{13... | collective-permute-start | bytes 53768 | tf_op jit(solution)/shard_map/ppermute | solution.py:22
  32.6 3.1 %collective-permute-start.1 = (bf16[128,35,2]{0,2,1:T(2,128)(2,1)S(1)}, bf16[128,35,2]{0,2,1:T(2,128)(2,1)S(1)}, u32[]{:S(2)}, u32[]{:S(2)}) collective-permute-start(bf16[128,35,2]{0,2,1:T(2,128)(2,1)S(1)} %get-tuple-element.86), channel_id=1, source_target_pairs={{0,4},{4,8},{8,12},{12,16},{16,20},{20,24},{24,28},{1,5},{5,9},{9,... | collective-permute-start | bytes 53768 | tf_op jit(solution)/shard_map/ppermute | solution.py:19
  38.7 3.6 %copy.58 = bf16[128,35,132]{2,1,0:T(8,128)(2,1)S(1)} copy(bf16[128,35,132]{0,2,1:T(8,128)(2,1)} %pad_maximum_fusion.8) | data formatting | bytes 2365440 | tf_op jit(solution)/shard_map/concatenate | solution.py:23
  42.3 5.4 %collective-permute-start.3 = (bf16[2,35,132]{2,1,0:T(8,128)(2,1)S(1)}, bf16[2,35,132]{2,1,0:T(8,128)(2,1)S(1)}, u32[]{:S(2)}, u32[]{:S(2)}) collective-permute-start(bf16[2,35,132]{2,1,0:T(8,128)(2,1)S(1)} %get-tuple-element.84), channel_id=1, source_target_pairs={{0,1},{1,2},{2,3},{4,5},{5,6},{6,7},{8,9},{9,10},{10,11},{12,13},{... | collective-permute-start | bytes 55448 | tf_op jit(solution)/shard_map/ppermute | solution.py:19
  53.1 2.9 %fusion.110 = f32[130,130,32]{1,2,0:T(8,128)} fusion(bf16[2,35,132]{2,1,0:T(8,128)(2,1)S(1)} %collective-permute-done.4, bf16[128,35,132]{2,1,0:T(8,128)(2,1)S(1)} %copy.58, bf16[2,35,132]{2,1,0:T(8,128)(2,1)S(1)} %collective-permute-done.3, bf16[3,3,32,3]{2,3,1,0:T(4,128)(2,1)S(1)} %copy-done.6), kind=kOutput, calls=%fused_computation.140 | convolution fusion | flops 3549000 | bytes 4867584 | tf_op jit(solution)/shard_map/oi,xiy->xoy/dot_general | solution.py:37
  56.0 2.8 %fusion.120 = f32[130,130,32]{1,2,0:T(8,128)} fusion(bf16[2,35,132]{2,1,0:T(8,128)(2,1)S(1)} %collective-permute-done.4, bf16[128,35,132]{2,1,0:T(8,128)(2,1)S(1)} %copy.58, bf16[3,3,32,3]{2,3,1,0:T(4,128)(2,1)S(1)} %copy-done.6), kind=kOutput, calls=%fused_computation.150 | convolution fusion | flops 3447600 | bytes 4826624 | tf_op jit(solution)/shard_map/oi,xiy->xoy/dot_general | solution.py:37
  58.8 2.8 %fusion.124 = f32[130,130,32]{1,2,0:T(8,128)} fusion(bf16[2,35,132]{2,1,0:T(8,128)(2,1)S(1)} %collective-permute-done.4, bf16[128,35,132]{2,1,0:T(8,128)(2,1)S(1)} %copy.58, bf16[2,35,132]{2,1,0:T(8,128)(2,1)S(1)} %collective-permute-done.3, bf16[3,3,32,3]{2,3,1,0:T(4,128)(2,1)S(1)} %copy-done.6), kind=kOutput, calls=%fused_computation.154 | convolution fusion | flops 3549000 | bytes 4867584 | tf_op jit(solution)/shard_map/oi,xiy->xoy/dot_general | solution.py:37
  64.3 2.7 %fusion.134 = f32[130,130,32]{1,2,0:T(8,128)} fusion(bf16[2,35,132]{2,1,0:T(8,128)(2,1)S(1)} %collective-permute-done.4, bf16[128,35,132]{2,1,0:T(8,128)(2,1)S(1)} %copy.58, bf16[3,3,32,3]{2,3,1,0:T(4,128)(2,1)S(1)} %copy-done.6), kind=kOutput, calls=%fused_computation.164 | convolution fusion | flops 3447600 | bytes 4826624 | tf_op jit(solution)/shard_map/oi,xiy->xoy/dot_general | solution.py:37
  67.1 2.8 %fusion.144 = f32[130,130,32]{1,2,0:T(8,128)} fusion(bf16[128,35,132]{2,1,0:T(8,128)(2,1)S(1)} %copy.58, bf16[2,35,132]{2,1,0:T(8,128)(2,1)S(1)} %collective-permute-done.3, bf16[3,3,32,3]{2,3,1,0:T(4,128)(2,1)S(1)} %copy-done.6), kind=kOutput, calls=%fused_computation.174 | convolution fusion | flops 3447600 | bytes 4826624 | tf_op jit(solution)/shard_map/oi,xiy->xoy/dot_general | solution.py:37
  69.9 2.8 %fusion.138 = f32[130,130,32]{1,2,0:T(8,128)} fusion(bf16[2,35,132]{2,1,0:T(8,128)(2,1)S(1)} %collective-permute-done.4, bf16[128,35,132]{2,1,0:T(8,128)(2,1)S(1)} %copy.58, bf16[2,35,132]{2,1,0:T(8,128)(2,1)S(1)} %collective-permute-done.3, bf16[3,3,32,3]{2,3,1,0:T(4,128)(2,1)S(1)} %copy-done.6), kind=kOutput, calls=%fused_computation.168 | convolution fusion | flops 3549000 | bytes 4867584 | tf_op jit(solution)/shard_map/oi,xiy->xoy/dot_general | solution.py:37
  72.7 14.8 %fusion.34 = (bf16[130,32,130]{2,1,0:T(8,128)(2,1)S(1)}, f32[130,130,32]{1,2,0:T(8,128)}) fusion(pred[130,130]{1,0:T(8,128)(4,1)S(1)} %broadcast_and_fusion, f32[32]{0:T(128)S(1)} %copy-done.8, bf16[3,3,32,3]{2,3,1,0:T(4,128)(2,1)S(1)} %copy-done.6, bf16[2,35,132]{2,1,0:T(8,128)(2,1)S(1)} %collective-permute-done.4, bf16[128,35,132]{2,1,0:T(8,128)(2,1)S(1)} %copy.58, ...), kind=kOutput, calls=%fused_computation.44 | convolution fusion | flops 11559600 | bytes 23249152 | tf_op jit(solution)/shard_map/oi,xiy->xoy/dot_general | solution.py:37
  102.0 3.2 %fusion.55 = f32[130,130,32]{1,2,0:T(8,128)} fusion(bf16[132,35,132]{2,1,0:T(8,128)(2,1)S(1)} %pad_maximum_fusion.1, bf16[3,3,32,32]{3,2,1,0:T(8,128)(2,1)S(1)} %copy-done.4), kind=kOutput, calls=%fused_computation.73 | convolution fusion | flops 34611200 | bytes 4301312 | tf_op jit(solution)/shard_map/oi,xoy->xiy/dot_general | solution.py:56
  105.2 3.2 %fusion.57 = f32[130,130,32]{1,2,0:T(8,128)} fusion(bf16[132,35,132]{2,1,0:T(8,128)(2,1)S(1)} %pad_maximum_fusion.1, bf16[3,3,32,32]{3,2,1,0:T(8,128)(2,1)S(1)} %copy-done.4), kind=kOutput, calls=%fused_computation.75 | convolution fusion | flops 34611200 | bytes 4301312 | tf_op jit(solution)/shard_map/oi,xoy->xiy/dot_general | solution.py:56
  108.3 2.8 %fusion.53 = f32[130,130,32]{1,2,0:T(8,128)} fusion(bf16[2,35,132]{2,1,0:T(8,128)(2,1)S(1)} %collective-permute-done.4, bf16[128,35,132]{2,1,0:T(8,128)(2,1)S(1)} %copy.58, bf16[3,3,32,32]{3,2,1,0:T(8,128)(2,1)S(1)} %copy-done.4), kind=kOutput, calls=%fused_computation.71 | convolution fusion | flops 36774400 | bytes 4833792 | tf_op jit(solution)/shard_map/oi,xoy->xiy/dot_general | solution.py:56
  111.2 3.7 %fusion.44 = f32[130,130,32]{1,2,0:T(8,128)} fusion(bf16[128,35,132]{2,1,0:T(8,128)(2,1)S(1)} %copy.58, bf16[2,35,132]{2,1,0:T(8,128)(2,1)S(1)} %collective-permute-done.3, bf16[3,3,32,32]{3,2,1,0:T(8,128)(2,1)S(1)} %copy-done.4), kind=kOutput, calls=%fused_computation.62 | convolution fusion | flops 35152000 | bytes 4833792 | tf_op jit(solution)/shard_map/oi,xoy->xiy/dot_general | solution.py:56
  114.8 3.6 %fusion.38 = f32[130,130,32]{1,2,0:T(8,128)} fusion(bf16[128,35,132]{2,1,0:T(8,128)(2,1)S(1)} %copy.58, bf16[2,35,132]{2,1,0:T(8,128)(2,1)S(1)} %collective-permute-done.4, bf16[3,3,32,32]{3,2,1,0:T(8,128)(2,1)S(1)} %copy-done.4), kind=kOutput, calls=%fused_computation.58 | convolution fusion | flops 35152000 | bytes 4833792 | tf_op jit(solution)/shard_map/oi,xoy->xiy/dot_general | solution.py:56
  118.4 4.0 %fusion.47 = f32[130,130,32]{1,2,0:T(8,128)} fusion(bf16[128,35,132]{2,1,0:T(8,128)(2,1)S(1)} %copy.58, bf16[2,35,132]{2,1,0:T(8,128)(2,1)S(1)} %collective-permute-done.3, bf16[3,3,32,32]{3,2,1,0:T(8,128)(2,1)S(1)} %copy-done.4), kind=kOutput, calls=%fused_computation.64 | convolution fusion | flops 35152000 | bytes 4833792 | tf_op jit(solution)/shard_map/oi,xoy->xiy/dot_general | solution.py:56
  122.4 3.7 %fusion.41 = f32[130,130,32]{1,2,0:T(8,128)} fusion(bf16[128,35,132]{2,1,0:T(8,128)(2,1)S(1)} %copy.58, bf16[2,35,132]{2,1,0:T(8,128)(2,1)S(1)} %collective-permute-done.4, bf16[3,3,32,32]{3,2,1,0:T(8,128)(2,1)S(1)} %copy-done.4), kind=kOutput, calls=%fused_computation.60 | convolution fusion | flops 35152000 | bytes 4833792 | tf_op jit(solution)/shard_map/oi,xoy->xiy/dot_general | solution.py:56
  126.1 13.8 %fusion.29 = bf16[130,32,130]{2,1,0:T(8,128)(2,1)S(1)} fusion(f32[130,130,32]{1,2,0:T(8,128)} %get-tuple-element.93, f32[130,130,32]{1,2,0:T(8,128)} %fusion.51, f32[130,130,32]{1,2,0:T(8,128)} %fusion.53, f32[130,130,32]{1,2,0:T(8,128)} %fusion.44, f32[130,130,32]{1,2,0:T(8,128)} %fusion.55, f32[130,130,32]{1,2,0:T(8,128)} %fusion.38, ...), kind=kOutput, calls=%fused_computation.36 | convolution fusion | flops 46508800 | bytes 23255808 | tf_op jit(solution)/shard_map/oi,xoy->xiy/dot_general | solution.py:56
  143.7 3.0 %collective-permute-start.5 = (bf16[128,2,128]{2,1,0:T(2,128)(2,1)S(1)}, bf16[128,2,128]{2,1,0:T(2,128)(2,1)S(1)}, u32[]{:S(2)}, u32[]{:S(2)}) collective-permute-start(bf16[128,2,128]{2,1,0:T(2,128)(2,1)S(1)} %bitcast.290), channel_id=1, source_target_pairs={{4,0},{8,4},{12,8},{16,12},{20,16},{24,20},{28,24},{5,1},{9,5},{13... | collective-permute-start | bytes 196616 | tf_op jit(solution)/shard_map/ppermute | solution.py:11
  154.4 7.2 %fusion.62 = bf16[128,32,128]{2,1,0:T(8,128)(2,1)} fusion(f32[128,128,32]{1,2,0:T(8,128)S(1)} %copy-done.1, f32[128,128,32]{1,2,0:T(8,128)S(1)} %copy-done.2, f32[128,128,32]{1,2,0:T(8,128)} %fusion.83, f32[128,128,32]{1,2,0:T(8,128)} %fusion.85, f32[128,128,32]{1,2,0:T(8,128)} %fusion.87, f32[128,128,32]{1,2,0:T(8,128)} %fusion.89, ...), kind=kOutput, calls=%fused_computation.82 | convolution fusion | flops 38797312 | bytes 18883072 | tf_op jit(solution)/shard_map/oi,xiy->xoy/dot_general | solution.py:37
  (149 shorter events, 57.6 us)
Async XLA Ops:
  9.3 17.3 %copy-start.5 = (s32[1024,4]{0,1:T(4,128)S(1)}, s32[1024,4]{0,1:T(4,128)}, u32[]{:S(2)}) copy-start(s32[1024,4]{0,1:T(4,128)} %param.10) | copy-start | bytes 49156
  9.3 17.3 %copy-start.3 = (bf16[128,32,128]{2,1,0:T(8,128)(2,1)S(1)}, bf16[128,32,128]{2,1,0:T(8,128)(2,1)}, u32[]{:S(2)}) copy-start(bf16[128,32,128]{2,1,0:T(8,128)(2,1)} %param.17) | copy-start | bytes 3145732
  23.3 6.1 %collective-permute-start = (bf16[128,3,128]{0,2,1:T(8,128)(2,1)S(1)}, bf16[128,3,128]{0,2,1:T(8,128)(2,1)S(1)}, u32[]{:S(2)}, u32[]{:S(2)}) collective-permute-start(bf16[128,3,128]{0,2,1:T(8,128)(2,1)S(1)} %fusion.150), channel_id=1, source_target_pairs={{0,4},{4,8},{8,12},{12,16},{16,20},{20,24},{24,28},{1,5},{5,9},{9,... | collective-permute-start | bytes 294920 | tf_op jit(solution)/shard_map/ppermute | solution.py:11
  29.5 6.2 %collective-permute-start.2 = (bf16[128,35,2]{0,2,1:T(2,128)(2,1)S(1)}, bf16[128,35,2]{0,2,1:T(2,128)(2,1)S(1)}, u32[]{:S(2)}, u32[]{:S(2)}) collective-permute-start(bf16[128,35,2]{0,2,1:T(2,128)(2,1)S(1)} %get-tuple-element.87), channel_id=1, source_target_pairs={{4,0},{8,4},{12,8},{16,12},{20,16},{24,20},{28,24},{5,1},{9,5},{13... | collective-permute-start | bytes 53768 | tf_op jit(solution)/shard_map/ppermute | solution.py:22
  32.6 4.5 %collective-permute-start.1 = (bf16[128,35,2]{0,2,1:T(2,128)(2,1)S(1)}, bf16[128,35,2]{0,2,1:T(2,128)(2,1)S(1)}, u32[]{:S(2)}, u32[]{:S(2)}) collective-permute-start(bf16[128,35,2]{0,2,1:T(2,128)(2,1)S(1)} %get-tuple-element.86), channel_id=1, source_target_pairs={{0,4},{4,8},{8,12},{12,16},{16,20},{20,24},{24,28},{1,5},{5,9},{9,... | collective-permute-start | bytes 53768 | tf_op jit(solution)/shard_map/ppermute | solution.py:19
  35.7 14.2 %copy-start.6 = (bf16[3,3,32,3]{2,3,1,0:T(4,128)(2,1)S(1)}, bf16[3,3,32,3]{2,3,1,0:T(4,128)(2,1)}, u32[]{:S(2)}) copy-start(bf16[3,3,32,3]{2,3,1,0:T(4,128)(2,1)} %param.13) | copy-start | bytes 5188
  42.3 7.6 %collective-permute-start.3 = (bf16[2,35,132]{2,1,0:T(8,128)(2,1)S(1)}, bf16[2,35,132]{2,1,0:T(8,128)(2,1)S(1)}, u32[]{:S(2)}, u32[]{:S(2)}) collective-permute-start(bf16[2,35,132]{2,1,0:T(8,128)(2,1)S(1)} %get-tuple-element.84), channel_id=1, source_target_pairs={{0,1},{1,2},{2,3},{4,5},{5,6},{6,7},{8,9},{9,10},{10,11},{12,13},{... | collective-permute-start | bytes 55448 | tf_op jit(solution)/shard_map/ppermute | solution.py:19
  47.8 5.3 %collective-permute-start.4 = (bf16[2,35,132]{2,1,0:T(8,128)(2,1)S(1)}, bf16[2,35,132]{2,1,0:T(8,128)(2,1)S(1)}, u32[]{:S(2)}, u32[]{:S(2)}) collective-permute-start(bf16[2,35,132]{2,1,0:T(8,128)(2,1)S(1)} %get-tuple-element.85), channel_id=1, source_target_pairs={{1,0},{2,1},{3,2},{5,4},{6,5},{7,6},{9,8},{10,9},{11,10},{13,12},{... | collective-permute-start | bytes 55448 | tf_op jit(solution)/shard_map/ppermute | solution.py:22
  69.8 2.8 %copy-start.8 = (f32[32]{0:T(128)S(1)}, f32[32]{0:T(128)}, u32[]{:S(2)}) copy-start(f32[32]{0:T(128)} %param.14) | copy-start | bytes 388
  72.7 14.8 %copy-start.4 = (bf16[3,3,32,32]{3,2,1,0:T(8,128)(2,1)S(1)}, bf16[3,3,32,32]{3,2,1,0:T(8,128)(2,1)}, u32[]{:S(2)}) copy-start(bf16[3,3,32,32]{3,2,1,0:T(8,128)(2,1)} %param.15) | copy-start | bytes 55300
  87.5 59.3 %copy-start = (bf16[130,32,130]{2,1,0:T(8,128)(2,1)}, bf16[130,32,130]{2,1,0:T(8,128)(2,1)S(1)}, u32[]{:S(2)}) copy-start(bf16[130,32,130]{2,1,0:T(8,128)(2,1)S(1)} %get-tuple-element.92) | copy-start | bytes 3244804
  143.7 5.9 %collective-permute-start.5 = (bf16[128,2,128]{2,1,0:T(2,128)(2,1)S(1)}, bf16[128,2,128]{2,1,0:T(2,128)(2,1)S(1)}, u32[]{:S(2)}, u32[]{:S(2)}) collective-permute-start(bf16[128,2,128]{2,1,0:T(2,128)(2,1)S(1)} %bitcast.290), channel_id=1, source_target_pairs={{4,0},{8,4},{12,8},{16,12},{20,16},{24,20},{28,24},{5,1},{9,5},{13... | collective-permute-start | bytes 196616 | tf_op jit(solution)/shard_map/ppermute | solution.py:11
  148.5 5.9 %copy-start.1 = (f32[128,128,32]{1,2,0:T(8,128)S(1)}, f32[128,128,32]{1,2,0:T(8,128)}, u32[]{:S(2)}) copy-start(f32[128,128,32]{1,2,0:T(8,128)} %fusion.79) | copy-start | bytes 6291460
  148.5 5.9 %copy-start.7 = (f32[32]{0:T(128)S(1)}, f32[32]{0:T(128)}, u32[]{:S(2)}) copy-start(f32[32]{0:T(128)} %param.16) | copy-start | bytes 388
  150.0 4.4 %copy-start.2 = (f32[128,128,32]{1,2,0:T(8,128)S(1)}, f32[128,128,32]{1,2,0:T(8,128)}, u32[]{:S(2)}) copy-start(f32[128,128,32]{1,2,0:T(8,128)} %fusion.81) | copy-start | bytes 6291460
  150.0 1.9 %collective-permute-start.6 = (bf16[128,512]{0,1:T(8,128)(2,1)S(1)}, bf16[128,512]{0,1:T(8,128)(2,1)S(1)}, u32[]{:S(2)}, u32[]{:S(2)}) collective-permute-start(bf16[128,512]{0,1:T(8,128)(2,1)S(1)} %bitcast.284), channel_id=1, source_target_pairs={{0,1},{1,0},{2,3},{3,2},{4,5},{5,4},{6,7},{7,6},{8,9},{9,8},{10,11... | collective-permute-start | bytes 393224 | tf_op jit(solution)/shard_map/ppermute | solution.py:163
  151.9 9.7 %collective-permute-start.7 = (bf16[256,512]{0,1:T(8,128)(2,1)S(1)}, bf16[256,512]{0,1:T(8,128)(2,1)S(1)}, u32[]{:S(2)}, u32[]{:S(2)}) collective-permute-start(bf16[256,512]{0,1:T(8,128)(2,1)S(1)} %maximum_select_fusion.2), channel_id=1, source_target_pairs={{0,2},{1,3},{2,0},{3,1},{4,6},{5,7},{6,4},{7,5},{8,10},{9,11},{10,... | collective-permute-start | bytes 786440 | tf_op jit(solution)/shard_map/ppermute | solution.py:163
